TPU v7x, 128 devices: a whole 4x4x4 slice. The times are simulated.
128 devices in a mesh: item: 4 (over x), row: 16 (over z, y), col: 2 (over core).
Axes of the slice: x: 4, y: 4, z: 4, core: 2. Of those that a mesh axis runs over, the one named last changes fastest.
Arguments:
- img_hidden: bfloat16 [32, 1024, 3072], P('item', ('row', 'col')), parts along dimension 0, may hold values from -1.796875 to 1.796875
- text_hidden: bfloat16 [32, 512, 3072], P('item', ('row', 'col')), parts along dimension 0, may hold values from -1.796875 to 1.796875
- latent: float32 [32, 1024, 64], P('item', ('row', 'col')), parts along dimension 0, may hold values from -6 to 6
- text_len: int32 [32], P('item'), parts along dimension 0, may hold values from 1 to 512, as said below
- block_keep: int32 [32, 16], P('item'), parts along dimension 0, may hold values 0 or 1
- img_pos: int32 [1024, 3], P(('row', 'col')), may hold values from 0 to 62, as said below
- modulation: float32 [32, 5, 3072], P('item'), parts along dimension 0, may hold values from -4 to 4
- qk_gain: float32 [2, 128], replicated, may hold values from 0.7 to 7
- w_qkv: bfloat16 [3072, 3, 1536], P(None, None, 'col'), may hold values from -0.109375 to 0.109375
- w_out: bfloat16 [1536, 3072], P('col'), may hold values from -0.25 to 0.25
- w_final: bfloat16 [3072, 64], replicated, may hold values from -0.109375 to 0.109375
Outputs:
- img_out: bfloat16 [32, 1024, 3072], P('item', ('row', 'col')), parts along dimension 0
- text_out: bfloat16 [32, 512, 3072], P('item', ('row', 'col')), parts along dimension 0
- latent_next: float32 [32, 1024, 64], P('item', ('row', 'col')), parts along dimension 0
There are 4 independent parts, one for each index of `item`. A program takes and returns all parts, laid end to end along the dimension named above; an argument that names none is the same for every part. Nothing has to cross between parts.
Inputs may be any that keep to these rules, and one draw needn't show every extreme that they name: `text_len`: at least one sample of every request uses all 512 text slots. `img_pos`: image token i, in image row r = i // 32 and column q = i % 32, has ids (c_i, a_r + r, b_q + q), where every token has its own frame id c_i of 0 to 3, every image row its own offset a_r and every image column its own offset b_q, each of 0 to 31.
All inputs are finite; a program needn't handle non-finite values.
Results may differ from a plain program's by a relative error of at most 0.015.
The roundings to bfloat16 on the way count: a program that leaves them out, or rounds other values in their place, can miss the bound.
Values may be sent and summed in bfloat16 or wider, within the bound.
No kernel may reach another device: no remote copies, remote signals or barrier semaphores. Data moves between devices by JAX's collectives and lax.ppermute only.
A program may use at most 256 MiB of HBM per device.

v0:
```python
import jax
import jax.numpy as jnp
import numpy as np
from jax import lax
from jax.sharding import PartitionSpec as P

KBLK = 64
eps_norm = 1e-06
theta_base = 10000.0
step_size = -0.25


def layer_norm(values):
    center = values - jnp.mean(values, axis=-1, keepdims=True)
    return center * lax.rsqrt(jnp.mean(center * center, axis=-1, keepdims=True) + eps_norm)


def modulate(hidden, shift, scale):
    return ((1.0 + scale) * layer_norm(hidden.astype(jnp.float32)) + shift).astype(jnp.bfloat16)


def rope_tables(head_dim):
    half = head_dim // 2
    first = head_dim // 16
    second = (half - first) // 2
    counts = [first, second, half - first - second]
    tables = []
    for axis_id in range(3):
        pieces = []
        for other in range(3):
            if other == axis_id:
                pieces.append(theta_base ** (-np.arange(counts[other]) / counts[other]))
            else:
                pieces.append(np.zeros(counts[other]))
        tables.append(np.concatenate(pieces).astype(np.float32))
    return tables


def angles_of(positions, head_dim):
    tables = rope_tables(head_dim)
    angle = positions[:, 0:1] * jnp.asarray(tables[0]) + positions[:, 1:2] * jnp.asarray(tables[1])
    angle = angle + positions[:, 2:3] * jnp.asarray(tables[2])
    return (jnp.cos(angle), jnp.sin(angle))


def rotate(values, cosine, sine):
    half = values.shape[-1] // 2
    first_half = values[..., :half]
    second_half = values[..., half:]
    cos_rows = cosine[:, None, :]
    sin_rows = sine[:, None, :]
    return jnp.concatenate(
        [
            first_half * cos_rows - second_half * sin_rows,
            second_half * cos_rows + first_half * sin_rows,
        ],
        axis=-1,
    )


def rms_gain(values, gain):
    return values * lax.rsqrt(jnp.mean(values * values, axis=-1, keepdims=True) + eps_norm) * gain


def valid_keys(text_len, block_keep, count, text_rows, img_rows):
    group = text_rows + img_rows
    index = jnp.arange(count, dtype=jnp.int32)
    device = index // group
    local = index % group
    is_text = local < text_rows
    text_index = device * text_rows + local
    img_index = device * img_rows + jnp.maximum(local - text_rows, 0)
    text_ok = text_index[None, :] < text_len[:, None]
    onehot = (
        (img_index // KBLK)[:, None] == jnp.arange(block_keep.shape[1], dtype=jnp.int32)[None, :]
    ).astype(jnp.int32)
    img_ok = jnp.sum(block_keep[:, None, :] * onehot[None], axis=-1) > 0
    return jnp.where(is_text[None, :], text_ok, img_ok)


def absorb(state, piece, valid, query):
    top, total, summed = state
    key_piece, value_piece = piece
    samples = key_piece.shape[0]
    count = key_piece.shape[1]
    heads = query.shape[2]
    head_dim = query.shape[3]
    key_split = key_piece.reshape(samples, count, heads, head_dim)
    value_split = value_piece.reshape(samples, count, heads, head_dim)
    scores = jnp.einsum(
        "sqhd,skhd->shqk", query, key_split, preferred_element_type=jnp.float32
    ) * head_dim ** (-0.5)
    scores = jnp.where(valid[:, None, None, :], scores, -jnp.inf)
    new_top = jnp.maximum(top, jnp.max(scores, axis=-1))
    weights = jnp.exp(scores - new_top[..., None])
    factor = jnp.exp(top - new_top)
    total = total * factor + jnp.sum(weights, axis=-1)
    summed = summed * factor[..., None] + jnp.einsum(
        "shqk,skhd->shqd",
        weights.astype(jnp.bfloat16),
        value_split,
        preferred_element_type=jnp.float32,
    )
    return (new_top, total, summed)


def per_device(
    img_hidden,
    text_hidden,
    latent,
    text_len,
    block_keep,
    img_pos,
    modulation,
    qk_gain,
    w_qkv,
    w_out,
    w_final,
):
    samples = img_hidden.shape[0]
    width = img_hidden.shape[2]
    head_dim = qk_gain.shape[1]
    local_inner = w_out.shape[0]
    local_heads = local_inner // head_dim
    mod_rows = modulation[:, :, None, :]
    text_norm = modulate(text_hidden, mod_rows[:, 0], mod_rows[:, 1])
    img_norm = modulate(img_hidden, mod_rows[:, 0], mod_rows[:, 1])
    text_group, img_group, pos_group = (
        lax.all_gather(text_norm, "col", axis=1, tiled=True),
        lax.all_gather(img_norm, "col", axis=1, tiled=True),
        lax.all_gather(img_pos.astype(jnp.bfloat16), "col", axis=0, tiled=True),
    )
    text_rows = text_group.shape[1]
    img_rows = img_group.shape[1]
    group = text_rows + img_rows
    joined = jnp.concatenate([text_group, img_group], axis=1)
    mixed = jnp.dot(
        joined.reshape(samples * group, width),
        w_qkv.reshape(width, 3 * local_inner),
        preferred_element_type=jnp.float32,
    )
    mixed = mixed.reshape(samples, group, 3, local_heads, head_dim)
    positions = jnp.concatenate(
        [jnp.zeros((text_rows, 3), jnp.float32), pos_group.astype(jnp.float32)], axis=0
    )
    cosine, sine = angles_of(positions, head_dim)
    query = rotate(rms_gain(mixed[:, :, 0], qk_gain[0]), cosine, sine).astype(jnp.bfloat16)
    keys = (
        rotate(rms_gain(mixed[:, :, 1], qk_gain[1]), cosine, sine)
        .astype(jnp.bfloat16)
        .reshape(samples, group, local_inner)
    )
    values = mixed[:, :, 2].astype(jnp.bfloat16).reshape(samples, group, local_inner)
    start_state = (
        jnp.full((samples, local_heads, group), -1e30, jnp.float32),
        jnp.zeros((samples, local_heads, group), jnp.float32),
        jnp.zeros((samples, local_heads, group, head_dim), jnp.float32),
    )
    piece = (
        lax.all_gather(keys, "row", axis=1, tiled=True),
        lax.all_gather(values, "row", axis=1, tiled=True),
    )
    count = piece[0].shape[1]
    valid = valid_keys(text_len, block_keep, count, text_rows, img_rows)
    top, total, summed = absorb(start_state, piece, valid, query)
    attention = jnp.transpose(summed / total[..., None], (0, 2, 1, 3)).astype(jnp.bfloat16)
    attention = attention.reshape(samples, group, local_inner)
    partial_sum = jnp.dot(
        attention.reshape(samples * group, local_inner), w_out, preferred_element_type=jnp.float32
    )
    partial_sum = partial_sum.reshape(samples, group, width)
    text_sum, img_sum = (
        lax.psum_scatter(
            partial_sum[:, :text_rows].astype(jnp.bfloat16), "col", scatter_dimension=1, tiled=True
        ).astype(jnp.float32),
        lax.psum_scatter(
            partial_sum[:, text_rows:].astype(jnp.bfloat16), "col", scatter_dimension=1, tiled=True
        ).astype(jnp.float32),
    )
    text_out = (text_hidden.astype(jnp.float32) + mod_rows[:, 2] * text_sum).astype(jnp.bfloat16)
    img_out = (img_hidden.astype(jnp.float32) + mod_rows[:, 2] * img_sum).astype(jnp.bfloat16)
    final = modulate(img_out, mod_rows[:, 3], mod_rows[:, 4])
    velocity = jnp.dot(
        final.reshape(samples * img_hidden.shape[1], width),
        w_final,
        preferred_element_type=jnp.float32,
    )
    velocity = velocity.reshape(samples, img_hidden.shape[1], w_final.shape[1])
    return (img_out, text_out, latent + step_size * velocity)


def solution(mesh):
    placed = (
        P("item", ("row", "col"), None),
        P("item", ("row", "col"), None),
        P("item", ("row", "col"), None),
        P("item"),
        P("item", None),
        P(("row", "col"), None),
        P("item", None, None),
        P(),
        P(None, None, "col"),
        P("col", None),
        P(),
    )
    return jax.shard_map(
        per_device,
        mesh=mesh,
        in_specs=placed,
        out_specs=(
            P("item", ("row", "col"), None),
            P("item", ("row", "col"), None),
            P("item", ("row", "col"), None),
        ),
        check_vma=False,
    )
```

profile of v0, /device:TPU:1, one launch (start us, length us, event | category | flops | bytes accessed | tf_op | source)
XLA Modules:
  0.0 409.7 jit_solution(13633441374526397716)
XLA Ops:
  7.2 1.3 fusion.55
  8.5 1.3 convert_reduce_fusion.2
  9.8 1.5 fusion.32
  11.3 1.3 fusion.35
  13.6 2.0 fusion.20
  15.7 18.7 %copy.38 = bf16[3072,3,768]{0,2,1:T(8,128)(2,1)} copy(bf16[3072,3,768]{2,0,1:T(8,128)(2,1)} %param.22) | data formatting | bytes 28311552 | tf_op args[8]
  34.4 3.0 all-gather
  37.8 9.6 %all-gather.8.cloned.1.call-done = bf16[8,64,3072]{2,1,0:T(8,128)(2,1)} async-done(((bf16[8,32,3072]{2,1,0:T(8,128)(2,1)}), bf16[8,64,3072]{2,1,0:T(8,128)(2,1)}) %all-gather.8.cloned.1.call-update) | async-done | bytes 3145744 | tf_op jit(solution)/shard_map/all_gather | solution.py:130
  47.4 14.7 %fusion.9 = f32[8,96,3,6,128]{4,1,3,2,0:T(8,128)S(1)} fusion(bf16[3,6,128,3072,1]{3,2,1,0,4:T(8,128)(2,1)} %bitcast.90, bf16[8,64,3072]{2,1,0:T(8,128)(2,1)} %all-gather.8.cloned.1.call-done, bf16[8,32,3072]{2,1,0:T(8,128)(2,1)} %all-gather.6.cloned.1.call-done), kind=kOutput, calls=%fused_computation.15 | convolution fusion | flops 10881073152 | bytes 25952256 | tf_op jit(solution)/shard_map/dot_general | solution.py:137
  62.1 1.7 multiply_reduce_fusion.1
  63.9 1.5 multiply_multiply_fusion.1
  65.4 2.8 subtract_convert_fusion.1
  68.2 1.6 copy_bitcast_fusion
  69.9 1.8 slice.129
  71.7 1.7 copy.44
  73.4 3.8 convert_element_type.70
  77.9 115.2 %all-gather.10.cloned.1.call-done = bf16[8,1536,768]{2,1,0:T(8,128)(2,1)} async-done(((bf16[8,96,768]{2,1,0:T(8,128)(2,1)}), bf16[8,1536,768]{2,1,0:T(8,128)(2,1)}) %all-gather.10.cloned.1.call-update) | async-done | bytes 18874384 | tf_op jit(solution)/shard_map/all_gather | solution.py:160
  193.0 24.9 %copy.42 = bf16[8,1536,768]{1,2,0:T(8,128)(2,1)} copy(bf16[8,1536,768]{2,1,0:T(8,128)(2,1)} %all-gather.10.cloned.1.call-done) | data formatting | bytes 37748736 | tf_op jit(solution)/shard_map/all_gather | solution.py:160
  217.9 16.8 %fusion = (f32[8,6,96]{2,1,0:T(8,128)S(1)}, f32[8,6,96,1536]{3,2,1,0:T(8,128)}) fusion(pred[8,1536]{1,0:T(8,128)(4,1)S(1)} %compare_select_fusion, bf16[8,1536,6,128]{1,3,2,0:T(8,128)(2,1)} %bitcast.88, bf16[8,96,6,64]{3,1,2,0:T(8,128)(2,1)} %get-tuple-element.10, bf16[8,96,6,64]{3,1,2,0:T(8,128)(2,1)} %get-tuple-element.9), kind=kOutput, calls=%fused_computation.2 | convolution fusion | flops 1835527680 | bytes 48396288 | tf_op jit(solution)/shard_map/sqhd,skhd->shqk/dot_general | solution.py:90
  234.7 11.8 %fusion.1 = f32[8,6,96]{2,1,0:T(8,128)S(1)} fusion(f32[8,6,96,1536]{3,2,1,0:T(8,128)} %get-tuple-element.30, f32[8,6,96]{2,1,0:T(8,128)S(1)} %get-tuple-element.21, pred[8,1536]{1,0:T(8,128)(4,1)S(1)} %compare_select_fusion), kind=kLoop, calls=%fused_computation.3 | loop fusion | flops 28306944 | bytes 28360704 | tf_op jit(solution)/shard_map/reduce_sum | solution.py:97
  246.5 70.3 %all-gather.12.cloned.1.call-done = bf16[8,1536,768]{2,1,0:T(8,128)(2,1)} async-done(((bf16[8,96,768]{2,1,0:T(8,128)(2,1)}), bf16[8,1536,768]{2,1,0:T(8,128)(2,1)}) %all-gather.12.cloned.1.call-update) | async-done | bytes 18874384 | tf_op jit(solution)/shard_map/all_gather | solution.py:161
  316.8 24.7 %copy.45 = bf16[8,1536,768]{1,2,0:T(8,128)(2,1)} copy(bf16[8,1536,768]{2,1,0:T(8,128)(2,1)} %all-gather.12.cloned.1.call-done) | data formatting | bytes 37748736 | tf_op jit(solution)/shard_map/all_gather | solution.py:161
  341.5 18.1 %fusion.39 = bf16[8,6,12,8,128]{4,3,2,1,0:T(8,128)(2,1)} fusion(bf16[8,1536,6,128]{1,3,2,0:T(8,128)(2,1)} %bitcast.89, f32[8,6,96,1536]{3,2,1,0:T(8,128)} %get-tuple-element.30, f32[8,6,96]{2,1,0:T(8,128)S(1)} %get-tuple-element.21, pred[8,1536]{1,0:T(8,128)(4,1)S(1)} %compare_select_fusion, f32[8,96,6]{1,2,0:T(8,128)S(1)} %bitcast_add_fusion.1, ...), kind=kOutput, calls=%fused_computation.59 | convolution fusion | flops 1842020352 | bytes 48433152 | tf_op jit(solution)/shard_map/shqk,skhd->shqd/dot_general | solution.py:98
  359.6 6.5 %convolution_convert_fusion = bf16[8,96,3072]{2,1,0:T(8,128)(2,1)S(1)} fusion(bf16[768,3072]{1,0:T(8,128)(2,1)} %param.23, bf16[8,6,12,8,128]{4,3,2,1,0:T(8,128)(2,1)} %fusion.39), kind=kOutput, calls=%fused_computation.10 | convolution fusion | flops 3626237952 | bytes 10616832 | tf_op jit(solution)/shard_map/dot_general | solution.py:168
  366.1 2.1 copy-done.5
  368.2 1.2 slice.93
  369.8 3.8 slice.92
  373.6 7.9 %reduce-scatter.5.cloned.1.call-done = bf16[8,16,3072]{2,1,0:T(8,128)(2,1)} async-done(((bf16[8,32,3072]{2,1,0:T(8,128)(2,1)}), bf16[8,16,3072]{2,1,0:T(8,128)(2,1)}) %reduce-scatter.5.cloned.1.call-update) | async-done | bytes 786448 | tf_op jit(solution)/shard_map/reduce_scatter | solution.py:173
  381.4 2.2 fusion.36
  383.7 15.0 %reduce-scatter.3.cloned.1.call-done = bf16[8,32,3072]{2,1,0:T(8,128)(2,1)} async-done(((bf16[8,64,3072]{2,1,0:T(8,128)(2,1)}), bf16[8,32,3072]{2,1,0:T(8,128)(2,1)}) %reduce-scatter.3.cloned.1.call-update) | async-done | bytes 1572880 | tf_op jit(solution)/shard_map/reduce_scatter | solution.py:176
  398.7 2.1 convert_reduce_fusion.1
  401.4 1.5 fusion.51
  (65 shorter events, 3.1 us)
Async XLA Ops:
  7.2 394.3 %copy-start = (bf16[3072,64]{0,1:T(8,128)(2,1)S(1)}, bf16[3072,64]{0,1:T(8,128)(2,1)}, u32[]{:S(2)}) copy-start(bf16[3072,64]{0,1:T(8,128)(2,1)} %param.24) | copy-start | bytes 1179652
  7.2 4.1 %copy-start.3 = (bf16[8,16,3072]{2,1,0:T(8,128)(2,1)S(1)}, bf16[8,16,3072]{2,1,0:T(8,128)(2,1)}, u32[]{:S(2)}) copy-start(bf16[8,16,3072]{2,1,0:T(8,128)(2,1)} %param.15) | copy-start | bytes 2359300
  7.2 30.6 %all-gather.6.cloned.1.call-start = ((), (), s32[]{:S(2)}) async-start(), calls=%async_computation.2 | async-start | bytes 2359296 | tf_op jit(solution)/shard_map/all_gather | solution.py:129
  7.2 5.5 %copy-start.1 = (bf16[8,32,3072]{2,1,0:T(8,128)(2,1)S(1)}, bf16[8,32,3072]{2,1,0:T(8,128)(2,1)}, u32[]{:S(2)}) copy-start(bf16[8,32,3072]{2,1,0:T(8,128)(2,1)} %param.14) | copy-start | bytes 4718596
  12.7 34.7 %all-gather.8.cloned.1.call-start = ((), (), s32[]{:S(2)}) async-start(), calls=%async_computation.3 | async-start | bytes 4718592 | tf_op jit(solution)/shard_map/all_gather | solution.py:130
  15.6 18.8 %copy-start.7 = (s32[32,3]{0,1:T(4,128)S(1)}, s32[32,3]{0,1:T(4,128)}, u32[]{:S(2)}) copy-start(s32[32,3]{0,1:T(4,128)} %param.19) | copy-start | bytes 1156
  15.6 21.9 %copy-start.8 = (f32[2,128]{1,0:T(2,128)S(1)}, f32[2,128]{1,0:T(2,128)}, u32[]{:S(2)}) copy-start(f32[2,128]{1,0:T(2,128)} %param.21) | copy-start | bytes 3076
  15.6 21.9 %copy-start.10 = (f32[64]{0:T(128)S(1)}, f32[64]{0:T(128)}, u32[]{:S(2)}) copy-start(f32[64]{0:T(128)} %constant.80.clone) | copy-start | bytes 772
  15.6 21.9 %copy-start.11 = (f32[64]{0:T(128)S(1)}, f32[64]{0:T(128)}, u32[]{:S(2)}) copy-start(f32[64]{0:T(128)} %constant.81.clone) | copy-start | bytes 772
  15.6 21.9 %copy-start.12 = (f32[64]{0:T(128)S(1)}, f32[64]{0:T(128)}, u32[]{:S(2)}) copy-start(f32[64]{0:T(128)} %constant.82.clone) | copy-start | bytes 772
  15.6 177.4 %all-gather.10.cloned.1.call-start = ((), (), s32[]{:S(2)}) async-start(), calls=%async_computation.4 | async-start | bytes 20054016 | tf_op jit(solution)/shard_map/all_gather | solution.py:160
  62.1 3.3 copy-start.2
  69.8 247.0 %all-gather.12.cloned.1.call-start = ((), (), s32[]{:S(2)}) async-start(), calls=%async_computation.5 | async-start | bytes 20054016 | tf_op jit(solution)/shard_map/all_gather | solution.py:161
  73.4 4.2 %copy-start.6 = (s32[8,16]{1,0:T(8,128)S(1)}, s32[8,16]{1,0:T(8,128)}, u32[]{:S(2)}) copy-start(s32[8,16]{1,0:T(8,128)} %param.18) | copy-start | bytes 1540
  73.4 4.4 %copy-start.9 = (s32[8]{0:T(128)S(1)}, s32[8]{0:T(128)}, u32[]{:S(2)}) copy-start(s32[8]{0:T(128)} %param.17) | copy-start | bytes 100
  77.2 304.2 %reduce-scatter.5.cloned.1.call-start = ((), (), s32[]{:S(2)}) async-start(), calls=%async_computation.7 | async-start | bytes 2359296 | tf_op jit(solution)/shard_map/reduce_scatter | solution.py:173
  366.1 2.1 copy-start.5
  369.5 29.2 %reduce-scatter.3.cloned.1.call-start = ((), (), s32[]{:S(2)}) async-start(), calls=%async_computation.6 | async-start | bytes 4718592 | tf_op jit(solution)/shard_map/reduce_scatter | solution.py:176
  383.7 17.8 %copy-start.13 = (f32[8,32,64]{2,1,0:T(8,128)S(1)}, f32[8,32,64]{2,1,0:T(8,128)}, u32[]{:S(2)}) copy-start(f32[8,32,64]{2,1,0:T(8,128)} %param.16) | copy-start | bytes 196612
  400.8 2.1 copy-start.4
Sparse Core Ops, SparseCore 0:
  12.8 16.1 all-gather.5
  31.2 16.1 all-gather.7
  70.0 123.0 all-gather.9
  195.0 121.7 all-gather.11
  369.6 11.7 reduce-scatter.4
  383.7 14.9 reduce-scatter.2
where the time goes:
time: 412 us; the launch traced here: 410 us
  waiting for transfers between devices  218 us (53%)
  local copies, waits for them, and re-layouts  82.8 us (20%)
  matrix products  57.6 us (14%)
  other arithmetic  33.3 us (8%)
  between operations  14.4 us (3%)
    all_gather x1, waiting for transfers between devices, per_device(): lax.all_gather(keys, 'row', axis=1, tiled=True)  115 us
    all_gather x1, waiting for transfers between devices, per_device(): lax.all_gather(values, 'row', axis=1, tiled=True)  70.3 us
    all_gather x1, local copies, waits for them, and re-layouts, per_device(): lax.all_gather(keys, 'row', axis=1, tiled=True)  24.9 us
    all_gather x1, local copies, waits for them, and re-layouts, per_device(): lax.all_gather(values, 'row', axis=1, tiled=True)  24.7 us
    unnamed x30, local copies, waits for them, and re-layouts  20.9 us
    dot_general x1, matrix products, absorb(): jnp.einsum('shqk,skhd->shqd', weights.astype(jnp.bfloat16), value_split,...  18.1 us
    dot_general x1, matrix products, absorb(): jnp.einsum('sqhd,skhd->shqk', query, key_split, preferred_element_type=jn...  16.8 us
    reduce_scatter x1, waiting for transfers between devices, per_device(): lax.psum_scatter(partial_sum[:, text_rows:].astype(jnp.bfloat16), 'col',...  15 us
  transfers between devices with their start and end apart: 6, of which 5 were waited for; matrix products, arithmetic and copies ran while one was open for 22% of the time, Pallas kernels for 0%

commit v1 on v0

--- a/solution.py
+++ b/solution.py
@@ -8,6 +8,16 @@
 eps_norm = 1e-06
 theta_base = 10000.0
 step_size = -0.25
+
+
+def raise_frame_all(own_rows, dev_axis):
+    local_part = jnp.concatenate(
+        lax.all_to_all(
+            jnp.stack([own_rows for _ in range(lax.axis_size(dev_axis))]), dev_axis, 0, 0
+        ),
+        axis=1,
+    )
+    return local_part
 
 
 def layer_norm(values):
@@ -156,10 +166,7 @@
         jnp.zeros((samples, local_heads, group), jnp.float32),
         jnp.zeros((samples, local_heads, group, head_dim), jnp.float32),
     )
-    piece = (
-        lax.all_gather(keys, "row", axis=1, tiled=True),
-        lax.all_gather(values, "row", axis=1, tiled=True),
-    )
+    piece = (lax.all_gather(keys, "row", axis=1, tiled=True), raise_frame_all(values, "row"))
     count = piece[0].shape[1]
     valid = valid_keys(text_len, block_keep, count, text_rows, img_rows)
     top, total, summed = absorb(start_state, piece, valid, query)

time: 412 us -> 629 us (1.53)
  waiting for transfers between devices: 218 us -> 393 us
  local copies, waits for them, and re-layouts: 82.8 us -> 119 us
  starting transfers between devices: 0.65 us -> 7.29 us
    all_to_all x0 -> x1, waiting for transfers between devices: none -> 335 us  [raise_frame_all(): lax.all_to_all(jnp.stack([own_rows for _ in range(lax.axis_size(dev_axis)...]
    all_gather x1, waiting for transfers between devices: 115 us -> 0.01 us  [per_device(): lax.all_gather(keys, 'row', axis=1, tiled=True)]
    all_gather x1 -> x0, waiting for transfers between devices: 70.3 us -> none  [per_device(): lax.all_gather(values, 'row', axis=1, tiled=True)]
    another operation x0 -> x2, local copies, waits for them, and re-layouts: none -> 47 us  [the longest x1 38.6 us: absorb(): value_split = value_piece.reshape(samples, count, heads, head_dim)]
    reduce_scatter x1, waiting for transfers between devices: 7.85 us -> 33.3 us  [per_device(): lax.psum_scatter(partial_sum[:, :text_rows].astype(jnp.bfloat16), 'col',...]
    all_gather x1 -> x0, local copies, waits for them, and re-layouts: 24.7 us -> none  [per_device(): lax.all_gather(values, 'row', axis=1, tiled=True)]
    reshape x0 -> x1, local copies, waits for them, and re-layouts: none -> 17.1 us  [raise_frame_all(): jnp.concatenate(lax.all_to_all(jnp.stack([own_rows for _ in range(lax.axi...]
    all_to_all x0 -> x1, starting transfers between devices: none -> 6.91 us  [raise_frame_all(): lax.all_to_all(jnp.stack([own_rows for _ in range(lax.axis_size(dev_axis)...]
  transfers between devices with their start and end apart: 6 -> 6, of which waited for: 5 -> 4; matrix products, arithmetic and copies ran while one was open for 22% -> 15% of each run, Pallas kernels for 0% -> 0%
where the time goes in v1:
time: 629 us; the launch traced here: 626 us
  waiting for transfers between devices  393 us (62%)
  local copies, waits for them, and re-layouts  119 us (19%)
  matrix products  57.2 us (9%)
  other arithmetic  32.3 us (5%)
  between operations  14.1 us (2%)
  starting transfers between devices  7.29 us (1%)
    all_to_all x1, waiting for transfers between devices, raise_frame_all(): lax.all_to_all(jnp.stack([own_rows for _ in range(lax.axis_size(dev_axis)...  335 us
    another operation x1, local copies, waits for them, and re-layouts, absorb(): value_split = value_piece.reshape(samples, count, heads, head_dim)  38.6 us
    reduce_scatter x1, waiting for transfers between devices, per_device(): lax.psum_scatter(partial_sum[:, :text_rows].astype(jnp.bfloat16), 'col',...  33.3 us
    all_gather x1, local copies, waits for them, and re-layouts, per_device(): lax.all_gather(keys, 'row', axis=1, tiled=True)  24.8 us
    unnamed x42, local copies, waits for them, and re-layouts  21 us
    dot_general x1, matrix products, absorb(): jnp.einsum('shqk,skhd->shqd', weights.astype(jnp.bfloat16), value_split,...  19.1 us
    reshape x1, local copies, waits for them, and re-layouts, raise_frame_all(): jnp.concatenate(lax.all_to_all(jnp.stack([own_rows for _ in range(lax.axi...  17.1 us
    dot_general x1, matrix products, absorb(): jnp.einsum('sqhd,skhd->shqk', query, key_split, preferred_element_type=jn...  15.3 us
  transfers between devices with their start and end apart: 6, of which 4 were waited for; matrix products, arithmetic and copies ran while one was open for 15% of the time, Pallas kernels for 0%

profile of v1, /device:TPU:1, one launch (start us, length us, event | category | flops | bytes accessed | tf_op | source)
XLA Modules:
  0.0 626.2 jit_solution(9242016070013237366)
XLA Ops:
  7.2 1.4 convert_reduce_fusion.2
  8.6 1.6 fusion.35
  10.2 1.8 fusion.60
  12.1 1.3 fusion.38
  14.3 2.0 fusion.21
  16.3 2.9 all-gather
  19.3 18.7 %copy.37 = bf16[3072,3,768]{0,2,1:T(8,128)(2,1)} copy(bf16[3072,3,768]{2,0,1:T(8,128)(2,1)} %param.22) | data formatting | bytes 28311552 | tf_op args[8]
  38.5 9.6 %all-gather.7.cloned.1.call-done = bf16[8,64,3072]{2,1,0:T(8,128)(2,1)} async-done(((bf16[8,32,3072]{2,1,0:T(8,128)(2,1)}), bf16[8,64,3072]{2,1,0:T(8,128)(2,1)}) %all-gather.7.cloned.1.call-update) | async-done | bytes 3145744 | tf_op jit(solution)/shard_map/all_gather | solution.py:140
  48.1 14.8 %fusion.10 = f32[8,96,3,6,128]{4,1,3,2,0:T(8,128)S(1)} fusion(bf16[3,6,128,3072,1]{3,2,1,0,4:T(8,128)(2,1)} %bitcast.90, bf16[8,64,3072]{2,1,0:T(8,128)(2,1)} %all-gather.7.cloned.1.call-done, bf16[8,32,3072]{2,1,0:T(8,128)(2,1)} %all-gather.5.cloned.1.call-done), kind=kOutput, calls=%fused_computation.16 | convolution fusion | flops 10881073152 | bytes 25952256 | tf_op jit(solution)/shard_map/dot_general | solution.py:147
  62.9 1.7 multiply_reduce_fusion.1
  64.6 1.5 multiply_multiply_fusion.1
  66.2 2.5 subtract_convert_fusion.1
  68.7 1.6 copy_bitcast_fusion
  70.4 1.8 slice.129
  72.7 2.2 convert_element_type.71
  74.9 8.4 %stack.3 = bf16[16,8,96,768]{3,2,1,0:T(8,128)(2,1)} broadcast(bf16[8,96,768]{2,1,0:T(8,128)(2,1)} %convert_element_type.71), dimensions={1,2,3} | broadcast | bytes 20054016 | tf_op jit(solution)/shard_map/stack | solution.py:16
  83.4 6.9 %all-to-all-start = ((bf16[16,8,96,768]{3,2,1,0:T(8,128)(2,1)}), bf16[16,8,96,768]{3,2,1,0:T(8,128)(2,1)}, u32[]{:S(2)}, u32[]{:S(2)}) async-start(bf16[16,8,96,768]{3,2,1,0:T(8,128)(2,1)} %stack.3), calls=%async_computation | async-start | bytes 37748736 | tf_op jit(solution)/shard_map/all_to_all | solution.py:15
  90.9 334.9 %all-to-all-done = bf16[16,8,96,768]{3,2,1,0:T(8,128)(2,1)} async-done(((bf16[16,8,96,768]{3,2,1,0:T(8,128)(2,1)}), bf16[16,8,96,768]{3,2,1,0:T(8,128)(2,1)}, u32[]{:S(2)}, u32[]{:S(2)}) %all-to-all-start) | async-done | bytes 18874400 | tf_op jit(solution)/shard_map/all_to_all | solution.py:15
  425.8 17.1 %copy.44 = bf16[8,16,96,768]{3,2,1,0:T(8,128)(2,1)} copy(bf16[8,16,96,768]{3,2,0,1:T(8,128)(2,1)} %bitcast.20) | data formatting | bytes 37748736 | tf_op jit(solution)/shard_map/reshape | solution.py:14
  443.0 38.6 %reshape_reshape.4 = bf16[8,1536,6,128]{3,2,1,0:T(8,128)(2,1)} reshape(bf16[8,16,96,768]{3,2,1,0:T(8,128)(2,1)} %copy.44) | data formatting | bytes 37748736 | tf_op jit(solution)/shard_map/reshape;reshape | solution.py:99
  481.6 24.8 %copy.41 = bf16[8,1536,768]{1,2,0:T(8,128)(2,1)} copy(bf16[8,1536,768]{2,1,0:T(8,128)(2,1)} %all-gather.9.cloned.1.call-done) | data formatting | bytes 37748736 | tf_op jit(solution)/shard_map/all_gather | solution.py:169
  506.3 15.3 %fusion = (f32[8,6,96]{2,1,0:T(8,128)S(1)}, f32[8,6,96,1536]{3,2,1,0:T(8,128)}) fusion(pred[8,1536]{1,0:T(8,128)(4,1)S(1)} %compare_select_fusion, bf16[8,1536,6,128]{1,3,2,0:T(8,128)(2,1)} %bitcast.89, bf16[8,96,6,64]{3,1,2,0:T(8,128)(2,1)S(1)} %copy-done.7, bf16[8,96,6,64]{3,1,2,0:T(8,128)(2,1)S(1)} %get-tuple-element.9), kind=kOutput, calls=%fused_computation.2 | convolution fusion | flops 1835527680 | bytes 48396288 | tf_op jit(solution)/shard_map/sqhd,skhd->shqk/dot_general | solution.py:100
  521.7 10.2 %fusion.1 = f32[8,6,96]{2,1,0:T(8,128)S(1)} fusion(f32[8,6,96,1536]{3,2,1,0:T(8,128)} %get-tuple-element.30, f32[8,6,96]{2,1,0:T(8,128)S(1)} %get-tuple-element.21, pred[8,1536]{1,0:T(8,128)(4,1)S(1)} %compare_select_fusion), kind=kLoop, calls=%fused_computation.3 | loop fusion | flops 28306944 | bytes 28360704 | tf_op jit(solution)/shard_map/reduce_sum | solution.py:107
  531.9 19.1 %fusion.42 = bf16[8,6,12,8,128]{4,3,2,1,0:T(8,128)(2,1)S(1)} fusion(bf16[8,1536,6,128]{3,2,1,0:T(8,128)(2,1)} %reshape_reshape.4, f32[8,6,96,1536]{3,2,1,0:T(8,128)} %get-tuple-element.30, f32[8,6,96]{2,1,0:T(8,128)S(1)} %get-tuple-element.21, pred[8,1536]{1,0:T(8,128)(4,1)S(1)} %compare_select_fusion, f32[8,96,6]{1,2,0:T(8,128)S(1)} %bitcast_add_fusion.1, ...), kind=kOutput, calls=%fused_computation.60 | convolution fusion | flops 1842020352 | bytes 48433152 | tf_op jit(solution)/shard_map/shqk,skhd->shqd/dot_general | solution.py:108
  551.1 6.5 %convolution_convert_fusion = bf16[8,96,3072]{2,1,0:T(8,128)(2,1)S(1)} fusion(bf16[768,3072]{1,0:T(8,128)(2,1)} %param.23, bf16[8,6,12,8,128]{4,3,2,1,0:T(8,128)(2,1)S(1)} %fusion.42), kind=kOutput, calls=%fused_computation.11 | convolution fusion | flops 3626237952 | bytes 10616832 | tf_op jit(solution)/shard_map/dot_general | solution.py:175
  557.6 2.1 copy-done.8
  561.0 3.7 slice.92
  564.8 33.3 %reduce-scatter.5.cloned.1.call-done = bf16[8,16,3072]{2,1,0:T(8,128)(2,1)} async-done(((bf16[8,32,3072]{2,1,0:T(8,128)(2,1)}), bf16[8,16,3072]{2,1,0:T(8,128)(2,1)}) %reduce-scatter.5.cloned.1.call-update) | async-done | bytes 786448 | tf_op jit(solution)/shard_map/reduce_scatter | solution.py:180
  598.1 2.3 fusion.39
  600.4 15.0 %reduce-scatter.3.cloned.1.call-done = bf16[8,32,3072]{2,1,0:T(8,128)(2,1)} async-done(((bf16[8,64,3072]{2,1,0:T(8,128)(2,1)}), bf16[8,32,3072]{2,1,0:T(8,128)(2,1)}) %reduce-scatter.3.cloned.1.call-update) | async-done | bytes 1572880 | tf_op jit(solution)/shard_map/reduce_scatter | solution.py:183
  615.4 2.1 convert_reduce_fusion.1
  618.2 1.5 fusion.56
  (78 shorter events, 4.6 us)
Async XLA Ops:
  7.2 611.0 %copy-start = (bf16[3072,64]{0,1:T(8,128)(2,1)S(1)}, bf16[3072,64]{0,1:T(8,128)(2,1)}, u32[]{:S(2)}) copy-start(bf16[3072,64]{0,1:T(8,128)(2,1)} %param.24) | copy-start | bytes 1179652
  7.2 4.9 copy-start.4
  7.2 31.3 %all-gather.5.cloned.1.call-start = ((), (), s32[]{:S(2)}) async-start(), calls=%async_computation.3 | async-start | bytes 2359296 | tf_op jit(solution)/shard_map/all_gather | solution.py:139
  8.6 4.8 copy-start.1
  13.4 34.7 %all-gather.7.cloned.1.call-start = ((), (), s32[]{:S(2)}) async-start(), calls=%async_computation.4 | async-start | bytes 4718592 | tf_op jit(solution)/shard_map/all_gather | solution.py:140
  14.3 2.0 copy-start.13
  16.3 465.3 %all-gather.9.cloned.1.call-start = ((), (), s32[]{:S(2)}) async-start(), calls=%async_computation.5 | async-start | bytes 20054016 | tf_op jit(solution)/shard_map/all_gather | solution.py:169
  19.3 18.8 %copy-start.14 = (f32[2,128]{1,0:T(2,128)S(1)}, f32[2,128]{1,0:T(2,128)}, u32[]{:S(2)}) copy-start(f32[2,128]{1,0:T(2,128)} %param.21) | copy-start | bytes 3076
  19.3 18.8 %copy-start.16 = (f32[64]{0:T(128)S(1)}, f32[64]{0:T(128)}, u32[]{:S(2)}) copy-start(f32[64]{0:T(128)} %constant.82.clone) | copy-start | bytes 772
  19.3 18.8 %copy-start.17 = (f32[64]{0:T(128)S(1)}, f32[64]{0:T(128)}, u32[]{:S(2)}) copy-start(f32[64]{0:T(128)} %constant.81.clone) | copy-start | bytes 772
  19.3 18.8 %copy-start.18 = (f32[64]{0:T(128)S(1)}, f32[64]{0:T(128)}, u32[]{:S(2)}) copy-start(f32[64]{0:T(128)} %constant.80.clone) | copy-start | bytes 772
  62.9 3.3 copy-start.3
  83.4 7.2 %copy-start.12 = (s32[8,16]{1,0:T(8,128)S(1)}, s32[8,16]{1,0:T(8,128)}, u32[]{:S(2)}) copy-start(s32[8,16]{1,0:T(8,128)} %param.18) | copy-start | bytes 1540
  83.4 7.5 %copy-start.15 = (s32[8]{0:T(128)S(1)}, s32[8]{0:T(128)}, u32[]{:S(2)}) copy-start(s32[8]{0:T(128)} %param.17) | copy-start | bytes 100
  83.4 342.5 %all-to-all-start = ((bf16[16,8,96,768]{3,2,1,0:T(8,128)(2,1)}), bf16[16,8,96,768]{3,2,1,0:T(8,128)(2,1)}, u32[]{:S(2)}, u32[]{:S(2)}) async-start(bf16[16,8,96,768]{3,2,1,0:T(8,128)(2,1)} %stack.3), calls=%async_computation | async-start | bytes 37748736 | tf_op jit(solution)/shard_map/all_to_all | solution.py:15
  90.3 507.8 %reduce-scatter.5.cloned.1.call-start = ((), (), s32[]{:S(2)}) async-start(), calls=%async_computation.7 | async-start | bytes 2359296 | tf_op jit(solution)/shard_map/reduce_scatter | solution.py:180
  481.6 24.8 %copy-start.7 = (bf16[8,96,6,64]{3,1,2,0:T(8,128)(2,1)S(1)}, bf16[8,96,6,64]{3,1,2,0:T(8,128)(2,1)}, u32[]{:S(2)}) copy-start(bf16[8,96,6,64]{3,1,2,0:T(8,128)(2,1)} %get-tuple-element.10) | copy-start | bytes 1769476
  557.6 2.1 copy-start.8
  561.0 54.4 %reduce-scatter.3.cloned.1.call-start = ((), (), s32[]{:S(2)}) async-start(), calls=%async_computation.6 | async-start | bytes 4718592 | tf_op jit(solution)/shard_map/reduce_scatter | solution.py:183
  564.8 33.3 %copy-start.5 = (bf16[8,16,3072]{2,1,0:T(8,128)(2,1)S(1)}, bf16[8,16,3072]{2,1,0:T(8,128)(2,1)}, u32[]{:S(2)}) copy-start(bf16[8,16,3072]{2,1,0:T(8,128)(2,1)} %param.15) | copy-start | bytes 2359300
  564.8 33.3 %copy-start.9 = (f32[8,3072]{1,0:T(8,128)S(1)}, f32[8,3072]{1,0:T(8,128)}, u32[]{:S(2)}) copy-start(f32[8,3072]{1,0:T(8,128)} %get-tuple-element.17) | copy-start | bytes 294916
  564.8 50.6 %copy-start.2 = (bf16[8,32,3072]{2,1,0:T(8,128)(2,1)S(1)}, bf16[8,32,3072]{2,1,0:T(8,128)(2,1)}, u32[]{:S(2)}) copy-start(bf16[8,32,3072]{2,1,0:T(8,128)(2,1)} %param.14) | copy-start | bytes 4718596
  600.4 17.8 %copy-start.10 = (f32[8,3072]{1,0:T(8,128)S(1)}, f32[8,3072]{1,0:T(8,128)}, u32[]{:S(2)}) copy-start(f32[8,3072]{1,0:T(8,128)} %get-tuple-element.13) | copy-start | bytes 294916
  600.4 17.8 %copy-start.11 = (f32[8,3072]{1,0:T(8,128)S(1)}, f32[8,3072]{1,0:T(8,128)}, u32[]{:S(2)}) copy-start(f32[8,3072]{1,0:T(8,128)} %get-tuple-element.14) | copy-start | bytes 294916
  600.4 17.8 %copy-start.19 = (f32[8,32,64]{2,1,0:T(8,128)S(1)}, f32[8,32,64]{2,1,0:T(8,128)}, u32[]{:S(2)}) copy-start(f32[8,32,64]{2,1,0:T(8,128)} %param.16) | copy-start | bytes 196612
  617.5 2.1 copy-start.6
Sparse Core Ops, SparseCore 0:
  13.5 16.1 all-gather.4
  31.9 16.1 all-gather.6
  70.5 377.1 all-gather.8
  561.1 36.9 reduce-scatter.4
  600.4 14.9 reduce-scatter.2
